TPU v7x, 32 devices: a whole 2x2x4 slice. The times are simulated.
32 devices in a mesh: mode: 8 (over z, y), space: 4 (over x, core).
Axes of the slice: x: 2, y: 2, z: 4, core: 2. Of those that a mesh axis runs over, the one named last changes fastest.
Arguments:
- modes: bfloat16 [3, 256, 16, 4, 128], P(None, 'mode', 'space'), may hold values from -6 to 6
- weights: float32 [16, 4, 128], P('space'), may hold values from 0.001275776 to 0.031894397
- plan: int32 [3], replicated, may hold values from 0 to 7, as said below
Outputs:
- convection: float32 [128, 32, 256], P('space', None, 'mode')
Inputs may be any that keep to these rules, and one draw needn't show every extreme that they name: plan[0] is 256 / 32 - 1, the last aligned block of 32 modes; plan[1] to plan[2] are distinct indices of aligned panels of 64 modes, below 256 / 64.
All inputs are finite; a program needn't handle non-finite values.
Results may differ from a plain program's by a relative error of at most 0.0041.
Values may be sent and summed in bfloat16 or wider, within the bound.
A program may use at most 128 MiB of HBM per device.

v0:
```python
import jax
import jax.numpy as jnp
from jax import lax
from jax.sharding import PartitionSpec as P

PANEL = 64
NPANEL = 2


def broadcast(value, axis, source):
    kept = jnp.where(lax.axis_index(axis) == source, value, 0).astype(value.dtype)
    return lax.psum(kept, axis)


def extended_2(array, sides, width):
    for axis, dim in sides:
        count, length = (lax.axis_size(axis), array.shape[dim])
        up = [(i, (i + 1) % count) for i in range(count)]
        down = [(j, i) for i, j in up]
        last = lax.slice_in_dim(array, length - width, length, axis=dim)
        first = lax.slice_in_dim(array, 0, width, axis=dim)
        before = lax.ppermute(last, axis, up)
        after = lax.ppermute(first, axis, down)
        array = jnp.concatenate([before, array, after], axis=dim)
    return array


def local(modes, weights, plan):
    local_modes = modes.shape[1]
    slabs_count = modes.shape[2]
    blocks_per_panel = PANEL // local_modes
    advecting = broadcast(modes, "mode", plan[0])
    pieces = []
    for panel in range(NPANEL):
        for half in range(blocks_per_panel):
            source = plan[1 + panel] * blocks_per_panel + half
            pieces.append(broadcast(modes, "mode", source))
    tests = jnp.concatenate(pieces, axis=1)
    test_count = tests.shape[1]
    weighted = (weights[None, None] * tests.astype(jnp.float32)).astype(jnp.bfloat16)
    weighted = weighted.reshape(3, test_count, -1)
    extended = extended_2(modes, (("space", 2),), 1)
    slabs = []
    for column in range(slabs_count):
        center = extended[:, :, column + 1].astype(jnp.float32)
        grad_x = 0.5 * (
            extended[:, :, column + 2].astype(jnp.float32)
            - extended[:, :, column].astype(jnp.float32)
        )
        grad_y = 0.5 * (jnp.roll(center, -1, axis=2) - jnp.roll(center, 1, axis=2))
        grad_z = 0.5 * (jnp.roll(center, -1, axis=3) - jnp.roll(center, 1, axis=3))
        advect = advecting[:, :, column].astype(jnp.float32)
        values = advect[0][None, :, None] * grad_x[:, None]
        values = values + advect[1][None, :, None] * grad_y[:, None]
        values = values + advect[2][None, :, None] * grad_z[:, None]
        slabs.append(values.astype(jnp.bfloat16))
    stacked = jnp.stack(slabs, axis=3)
    stacked = stacked.reshape(3, local_modes * local_modes, -1)
    own_rows = test_count // lax.axis_size("space")
    product = lax.dot_general(
        weighted, stacked, (((0, 2), (0, 2)), ((), ())), preferred_element_type=jnp.float32
    )
    return lax.psum_scatter(
        product.reshape(own_rows * lax.axis_size("space"), local_modes, local_modes),
        "space",
        scatter_dimension=0,
        tiled=True,
    )


def solution(mesh):
    in_specs = (P(None, "mode", "space", None, None), P("space", None, None), P())
    out_specs = P("space", None, "mode")
    return jax.shard_map(local, mesh=mesh, in_specs=in_specs, out_specs=out_specs, check_vma=False)
```

profile of v0, /device:TPU:1, one launch (start us, length us, event | category | flops | bytes accessed | tf_op | source)
XLA Modules:
  0.0 217.6 jit_solution(18249476317497189305)
XLA Ops:
  6.5 1.2 slice_bitcast_fusion.1
  7.7 2.6 %collective-permute-start = (bf16[3,32,1,4,128]{4,3,1,0,2:T(4,128)(2,1)S(1)}, bf16[3,32,1,4,128]{4,3,1,0,2:T(4,128)(2,1)S(1)}, u32[]{:S(2)}, u32[]{:S(2)}) collective-permute-start(bf16[3,32,1,4,128]{4,3,1,0,2:T(4,128)(2,1)S(1)} %get-tuple-element.14), channel_id=1, source_target_pairs={{0,1},{1,2},{2,3},{3,0},{4,5},{5,6},{6,7},{7,4},{8,9},{9,10},{10,1... | collective-permute-start | bytes 294920 | tf_op jit(solution)/shard_map/ppermute | solution.py:22
  10.4 1.4 fusion.37
  13.7 2.4 %broadcast_select_fusion.4 = (bf16[3,32,4,4,128]{4,3,2,1,0:T(4,128)(2,1)S(1)}, bf16[3,32,4,4,128]{4,3,2,1,0:T(4,128)(2,1)}, bf16[3,32,4,4,128]{4,3,2,1,0:T(4,128...) fusion(bf16[3,32,4,4,128]{4,3,2,1,0:T(4,128)(2,1)} %param.3, pred[]{:T(512)S(6)} %eq.15, ...), kind=kLoop, calls=%fused_computation.20 | loop fusion | flops 983040 | bytes 2359301 | tf_op jit(solution)/shard_map/jit(_where)/select_n | solution.py:11
  16.1 1.1 concatenate.128
  17.1 1.0 concatenate.131
  18.2 1.0 concatenate.130
  19.2 1.0 concatenate.129
  21.8 0.3 fusion.17
  22.0 0.3 fusion.15
  23.3 0.3 fusion.23
  23.6 0.3 fusion.13
  23.9 0.3 fusion.11
  24.4 96.4 %all-reduce.3.cloned.1.call-done = (bf16[3,32,4,4,128]{4,3,2,1,0:T(4,128)(2,1)}, bf16[3,32,2048]{2,1,0:T(8,128)(2,1)}, bf16[3,32,2048]{2,1,0:T(8,128)(2,1)}, bf1...) async-done(((bf16[3,32,4,4,128]{4,3,2,1,0:T(4,128)(2,1)}, bf16[3,32,2048]{2,1,0:T(8,128)(2,1)}, bf16[3,32,2048]{2,1,0:T(8,128)(2,1)}, bf16[3,32,2048]{2,1,0:T(8,128)(2,1)}, ...) | async-done | bytes 1966096 | tf_op jit(solution)/shard_map/psum | solution.py:12
  120.8 1.1 slice_convert_fusion.3
  122.0 2.5 %add_convert_fusion = bf16[3,32,32,1,4,128]{5,4,3,2,1,0:T(4,128)(2,1)S(1)} fusion(f32[3,32,4,128]{3,2,1,0:T(4,128)S(1)} %fusion.17, f32[32,4,128]{2,1,0:T(4,128)S(1)} %get-tuple-element.63, f32[3,32,4,128]{3,2,1,0:T(4,128)S(1)} %fusion.16, f32[32,4,128]{2,1,0:T(4,128)S(1)} %get-tuple-element.64, f32[3,32,4,128]{3,2,1,0:T(4,128)S(1)} %get-tuple-element.12, ...), kind=kLoop, calls=%fused_computation.1 | loop fusion | flops 9437184 | bytes 3932160 | tf_op jit(solution)/shard_map/convert_element_type | solution.py:56
  124.5 2.5 %add_convert_fusion.2 = bf16[3,32,32,1,4,128]{5,4,3,2,1,0:T(4,128)(2,1)S(1)} fusion(f32[3,32,4,128]{3,2,1,0:T(4,128)S(1)} %fusion.13, f32[32,4,128]{2,1,0:T(4,128)S(1)} %get-tuple-element.41, f32[3,32,4,128]{3,2,1,0:T(4,128)S(1)} %fusion.12, f32[32,4,128]{2,1,0:T(4,128)S(1)} %get-tuple-element.42, f32[3,32,4,128]{3,2,1,0:T(4,128)S(1)} %get-tuple-element.13, ...), kind=kLoop, calls=%fused_computation.3 | loop fusion | flops 9437184 | bytes 3932160 | tf_op jit(solution)/shard_map/convert_element_type | solution.py:56
  127.0 2.5 %add_convert_fusion.1 = bf16[3,32,32,1,4,128]{5,4,3,2,1,0:T(4,128)(2,1)S(1)} fusion(f32[3,32,4,128]{3,2,1,0:T(4,128)S(1)} %fusion.15, f32[32,4,128]{2,1,0:T(4,128)S(1)} %get-tuple-element.93, f32[3,32,4,128]{3,2,1,0:T(4,128)S(1)} %fusion.14, f32[32,4,128]{2,1,0:T(4,128)S(1)} %get-tuple-element.92, f32[3,32,4,128]{3,2,1,0:T(4,128)S(1)} %get-tuple-element.11, ...), kind=kLoop, calls=%fused_computation.2 | loop fusion | flops 9437184 | bytes 3932160 | tf_op jit(solution)/shard_map/convert_element_type | solution.py:56
  129.4 2.7 %add_convert_fusion.3 = bf16[3,32,32,1,4,128]{5,4,3,2,1,0:T(4,128)(2,1)S(1)} fusion(f32[3,32,4,128]{3,2,1,0:T(4,128)S(1)} %fusion.11, f32[32,4,128]{2,1,0:T(4,128)S(1)} %get-tuple-element.96, f32[3,32,4,128]{3,2,1,0:T(4,128)S(1)} %fusion.10, f32[32,4,128]{2,1,0:T(4,128)S(1)} %get-tuple-element.95, f32[3,32,4,128]{3,2,1,0:T(4,128)S(1)} %get-tuple-element.10, ...), kind=kLoop, calls=%fused_computation.4 | loop fusion | flops 9437184 | bytes 3932160 | tf_op jit(solution)/shard_map/convert_element_type | solution.py:56
  132.1 11.5 %pad_maximum_fusion = bf16[3,32,32,4,4,128]{5,4,3,2,1,0:T(4,128)(2,1)} fusion(bf16[3,32,32,1,4,128]{5,4,3,2,1,0:T(4,128)(2,1)S(1)} %add_convert_fusion, bf16[3,32,32,1,4,128]{5,4,3,2,1,0:T(4,128)(2,1)S(1)} %add_convert_fusion.1, bf16[3,32,32,1,4,128]{5,4,3,2,1,0:T(4,128)(2,1)S(1)} %add_convert_fusion.2, bf16[3,32,32,1,4,128]{5,4,3,2,1,0:T(4,128)(2,1)S(1)} %add_convert_fusion.3), kind=kLoop, calls=%fused_computation | loop fusion | flops 18874368 | bytes 25165824 | tf_op jit(solution)/shard_map/stack | solution.py:57
  143.7 21.2 %reshape.425 = bf16[3,1024,2048]{2,1,0:T(8,128)(2,1)} reshape(bf16[3,32,32,4,4,128]{5,4,3,2,1,0:T(4,128)(2,1)} %pad_maximum_fusion) | data formatting | bytes 25165824 | tf_op jit(solution)/shard_map/reshape | solution.py:58
  164.9 13.5 %convolution_bitcast_fusion = f32[128,32,32]{2,0,1:T(8,128)} fusion(bf16[32,32,3,2048]{3,1,0,2:T(8,128)(2,1)} %bitcast.81, bf16[3,32,2048]{2,1,0:T(8,128)(2,1)S(1)} %copy-done.1, bf16[3,32,2048]{2,1,0:T(8,128)(2,1)S(1)} %copy-done.2, bf16[3,32,2048]{2,1,0:T(8,128)(2,1)S(1)} %copy-done.3, bf16[3,32,2048]{2,1,0:T(8,128)(2,1)S(1)} %copy-done.4, ...), kind=kOutput, calls=%fused_computation.6 | convolution fusion | flops 1618477056 | bytes 14688256 | tf_op jit(solution)/shard_map/dot_general | solution.py:60
  178.4 30.2 %reduce-scatter.2.cloned.1.call-done = f32[32,32,32]{2,0,1:T(8,128)} async-done(((f32[128,32,32]{2,0,1:T(8,128)}), f32[32,32,32]{2,0,1:T(8,128)}) %reduce-scatter.2.cloned.1.call-update) | async-done | bytes 131088 | tf_op jit(solution)/shard_map/reduce_scatter | solution.py:63
  208.6 2.1 copy.14
  (33 shorter events, 2.8 us)
Async XLA Ops:
  6.5 114.3 %all-reduce.3.cloned.1.call-start = ((), (), s32[]{:S(2)}) async-start(), calls=%async_computation.2 | async-start | bytes 3932160 | tf_op jit(solution)/shard_map/psum | solution.py:12
  7.7 16.4 %collective-permute-start = (bf16[3,32,1,4,128]{4,3,1,0,2:T(4,128)(2,1)S(1)}, bf16[3,32,1,4,128]{4,3,1,0,2:T(4,128)(2,1)S(1)}, u32[]{:S(2)}, u32[]{:S(2)}) collective-permute-start(bf16[3,32,1,4,128]{4,3,1,0,2:T(4,128)(2,1)S(1)} %get-tuple-element.14), channel_id=1, source_target_pairs={{0,1},{1,2},{2,3},{3,0},{4,5},{5,6},{6,7},{7,4},{8,9},{9,10},{10,1... | collective-permute-start | bytes 294920 | tf_op jit(solution)/shard_map/ppermute | solution.py:22
  10.4 13.8 %collective-permute-start.1 = (bf16[3,32,1,4,128]{4,3,1,0,2:T(4,128)(2,1)S(1)}, bf16[3,32,1,4,128]{4,3,1,0,2:T(4,128)(2,1)S(1)}, u32[]{:S(2)}, u32[]{:S(2)}) collective-permute-start(bf16[3,32,1,4,128]{4,3,1,0,2:T(4,128)(2,1)S(1)} %get-tuple-element.17), channel_id=1, source_target_pairs={{1,0},{2,1},{3,2},{0,3},{5,4},{6,5},{7,6},{4,7},{9,8},{10,9},{11,1... | collective-permute-start | bytes 294920 | tf_op jit(solution)/shard_map/ppermute | solution.py:23
  20.3 188.3 %reduce-scatter.2.cloned.1.call-start = ((), (), s32[]{:S(2)}) async-start(), calls=%async_computation.1 | async-start | bytes 2621440 | tf_op jit(solution)/shard_map/reduce_scatter | solution.py:63
  21.4 2.8 %copy-start = (bf16[3,32,4,4,128]{4,3,2,1,0:T(4,128)(2,1)S(1)}, bf16[3,32,4,4,128]{4,3,2,1,0:T(4,128)(2,1)}, u32[]{:S(2)}) copy-start(bf16[3,32,4,4,128]{4,3,2,1,0:T(4,128)(2,1)} %param.3) | copy-start | bytes 1179652
  143.7 21.2 %copy-start.1 = (bf16[3,32,2048]{2,1,0:T(8,128)(2,1)S(1)}, bf16[3,32,2048]{2,1,0:T(8,128)(2,1)}, u32[]{:S(2)}) copy-start(bf16[3,32,2048]{2,1,0:T(8,128)(2,1)} %get-tuple-element.6) | copy-start | bytes 1179652
  143.7 21.2 %copy-start.2 = (bf16[3,32,2048]{2,1,0:T(8,128)(2,1)S(1)}, bf16[3,32,2048]{2,1,0:T(8,128)(2,1)}, u32[]{:S(2)}) copy-start(bf16[3,32,2048]{2,1,0:T(8,128)(2,1)} %get-tuple-element.7) | copy-start | bytes 1179652
  143.7 21.2 %copy-start.3 = (bf16[3,32,2048]{2,1,0:T(8,128)(2,1)S(1)}, bf16[3,32,2048]{2,1,0:T(8,128)(2,1)}, u32[]{:S(2)}) copy-start(bf16[3,32,2048]{2,1,0:T(8,128)(2,1)} %get-tuple-element.8) | copy-start | bytes 1179652
  143.7 21.2 %copy-start.4 = (bf16[3,32,2048]{2,1,0:T(8,128)(2,1)S(1)}, bf16[3,32,2048]{2,1,0:T(8,128)(2,1)}, u32[]{:S(2)}) copy-start(bf16[3,32,2048]{2,1,0:T(8,128)(2,1)} %get-tuple-element.9) | copy-start | bytes 1179652
  143.7 21.2 %copy-start.5 = (f32[4,4,128]{2,1,0:T(4,128)S(1)}, f32[4,4,128]{2,1,0:T(4,128)}, u32[]{:S(2)}) copy-start(f32[4,4,128]{2,1,0:T(4,128)} %param.4) | copy-start | bytes 24580
Sparse Core Ops, SparseCore 0:
  20.4 100.4 all-reduce.2
  178.5 29.9 reduce-scatter.1
where the time goes:
time: 219 us; the launch traced here: 218 us
  waiting for transfers between devices  127 us (58%)
  local copies, waits for them, and re-layouts  30.7 us (14%)
  other arithmetic  28.3 us (13%)
  between operations  15.5 us (7%)
  matrix products  13.5 us (6%)
  starting transfers between devices  2.87 us (1%)
    psum x1, waiting for transfers between devices, broadcast(): return lax.psum(kept, axis)  96.4 us
    reduce_scatter x1, waiting for transfers between devices, local(): lax.psum_scatter(product.reshape(own_rows * lax.axis_size('space'), local...  30.2 us
    reshape x1, local copies, waits for them, and re-layouts, local(): stacked = stacked.reshape(3, local_modes * local_modes, -1)  21.2 us
    dot_general x1, matrix products, local(): lax.dot_general(weighted, stacked, (((0, 2), (0, 2)), ((), ())), preferre...  13.5 us
    another operation x1, other arithmetic, local(): stacked = jnp.stack(slabs, axis=3)  11.5 us
    convert_element_type x4, other arithmetic, local(): slabs.append(values.astype(jnp.bfloat16))  10.1 us
  transfers between devices with their start and end apart: 4, of which 2 were waited for; matrix products, arithmetic and copies ran while one was open for 5% of the time, Pallas kernels for 0%

commit v1 on v0

v1 whole, which is shorter than its diff:
```python
import functools

import jax
import jax.numpy as jnp
from jax import lax
from jax.experimental import pallas as pl
from jax.experimental.pallas import tpu as pltpu
from jax.sharding import PartitionSpec as P

PANEL = 64
NPANEL = 2
MESH = pl.DeviceIdType.MESH
F32 = jnp.float32
BF16 = jnp.bfloat16


def kernel(dims, plan_ref, modes_ref, weights_ref, out_ref,
           ext, advb, up_in, dn_in, up_out, dn_out, tests, advf, vals, wts, acc, tot, stage, rs_in,
           halo_send, halo_recv, up_send, up_recv, dn_send, dn_recv, y_send, y_recv,
           ad_send, ay_send, adv_recv, rs_send, rs_recv):
    panels, spaces, cy, own_rows = dims
    comps, cells, nm, lanes = modes_ref.shape
    halves = 2
    hc = cells // halves
    chunks = comps * NPANEL * halves
    pairs = cells // 2
    quarter = pairs // 2
    last = panels - 1
    mode = lax.axis_index("mode")
    p = mode // 2
    q = lax.rem(mode, 2)
    me = lax.axis_index("space")
    partner = p * 2 + (1 - q)
    below = lax.rem(p + panels - 1, panels) * 2 + q
    above = lax.rem(p + 1, panels) * 2 + q
    right = lax.rem(me + 1, spaces)
    left = lax.rem(me + spaces - 1, spaces)
    is_src = jnp.logical_and(p == last, q == 1)
    not_src = jnp.logical_or(p < last, q == 0)

    barrier = pltpu.get_barrier_semaphore()
    for other in (partner, below, above):
        pl.semaphore_signal(barrier, inc=1, device_id={"mode": other}, device_id_type=MESH)
    for d in range(1, spaces):
        pl.semaphore_signal(barrier, inc=1, device_id={"space": lax.rem(me + d, spaces)}, device_id_type=MESH)

    def chunk_of(m):
        c = m // (NPANEL * halves)
        t = lax.rem(m // halves, NPANEL)
        h = lax.rem(m, halves)
        return c, t, h

    ext[:, cy : cy + cells] = modes_ref[...]

    @pl.when(is_src)
    def _():
        for a in range(pairs):
            advb[a] = modes_ref[:, 2 * a : 2 * a + 2]

    @pl.when(p == 0)
    def _():
        for m in range(chunks):
            c, t, h = m // (NPANEL * halves), (m // halves) % NPANEL, m % halves
            up_in[m] = modes_ref[c, h * hc : (h + 1) * hc]

    @pl.when(p == last)
    def _():
        for m in range(chunks):
            c, t, h = m // (NPANEL * halves), (m // halves) % NPANEL, m % halves
            dn_in[m] = modes_ref[c, h * hc : (h + 1) * hc]

    pl.semaphore_wait(barrier, 3 + spaces - 1)

    def copy_adv_down(a):
        return pltpu.make_async_remote_copy(
            src_ref=advb.at[q * quarter + a], dst_ref=advb.at[q * quarter + a],
            send_sem=ad_send.at[a], recv_sem=adv_recv.at[q * quarter + a],
            device_id={"mode": below}, device_id_type=MESH)

    def copy_adv_side(x):
        return pltpu.make_async_remote_copy(
            src_ref=advb.at[x], dst_ref=advb.at[x],
            send_sem=ay_send.at[x], recv_sem=adv_recv.at[x],
            device_id={"mode": partner}, device_id_type=MESH)

    def copy_up(m):
        return pltpu.make_async_remote_copy(
            src_ref=up_out.at[m], dst_ref=up_in.at[m], send_sem=up_send.at[m], recv_sem=up_recv.at[m],
            device_id={"mode": above}, device_id_type=MESH)

    def copy_down(m):
        return pltpu.make_async_remote_copy(
            src_ref=dn_out.at[m], dst_ref=dn_in.at[m], send_sem=dn_send.at[m], recv_sem=dn_recv.at[m],
            device_id={"mode": below}, device_id_type=MESH)

    def copy_side(m):
        return pltpu.make_async_remote_copy(
            src_ref=tests.at[m, q], dst_ref=tests.at[m, q], send_sem=y_send.at[m], recv_sem=y_recv.at[m],
            device_id={"mode": partner}, device_id_type=MESH)

    @pl.when(is_src)
    def _():
        for a in range(pairs):
            copy_adv_side(a).start()

    halo_up = pltpu.make_async_remote_copy(
        src_ref=modes_ref.at[:, pl.ds(cells - cy, cy)], dst_ref=ext.at[:, pl.ds(0, cy)],
        send_sem=halo_send.at[0], recv_sem=halo_recv.at[0], device_id={"space": right}, device_id_type=MESH)
    halo_down = pltpu.make_async_remote_copy(
        src_ref=modes_ref.at[:, pl.ds(0, cy)], dst_ref=ext.at[:, pl.ds(cells + cy, cy)],
        send_sem=halo_send.at[1], recv_sem=halo_recv.at[1], device_id={"space": left}, device_id_type=MESH)
    halo_up.start()
    halo_down.start()

    def values_of(xp):
        adv_at = advb.at[xp]
        for e in range(2):
            xy = 2 * xp + e
            x = xy // cy
            y = lax.rem(xy, cy)
            y_next = cy + x * cy + lax.rem(y + 1, cy)
            y_prev = cy + x * cy + lax.rem(y + cy - 1, cy)
            for d in range(3):
                advf[e, d] = adv_at[d, e].astype(F32)
            grads = []
            for c in range(comps):
                center = ext[c, xy + cy].astype(F32)
                gx = 0.5 * (ext[c, xy + 2 * cy].astype(F32) - ext[c, xy].astype(F32))
                gy = 0.5 * (ext[c, y_next].astype(F32) - ext[c, y_prev].astype(F32))
                gz = 0.5 * (pltpu.roll(center, lanes - 1, 1) - pltpu.roll(center, 1, 1))
                grads.append((gx, gy, gz))

            def row(j, carry):
                rows = [jnp.broadcast_to(advf[e, d, pl.ds(j, 1), :], (nm, lanes)) for d in range(3)]
                for c in range(comps):
                    value = rows[0] * grads[c][0] + rows[1] * grads[c][1] + rows[2] * grads[c][2]
                    start = pl.multiple_of(j * nm, nm)
                    vals[c * pairs + xp, pl.ds(start, nm), e * lanes : (e + 1) * lanes] = value.astype(BF16)
                return carry

            lax.fori_loop(0, nm, row, 0, unroll=4)

    ticks = chunks + quarter + last + 1

    def tick(step, carry):
        a = step - (last - p)

        @pl.when(jnp.logical_and(a >= 0, a < quarter))
        def _():
            @pl.when(not_src)
            def _():
                copy_adv_side(q * quarter + a).wait_recv()

            @pl.when(p > 0)
            def _():
                copy_adv_down(a).start()

            @pl.when(p < last)
            def _():
                copy_adv_side(q * quarter + a).start()

        mu = step - p

        @pl.when(jnp.logical_and(mu >= 0, mu < chunks))
        def _():
            @pl.when(p > 0)
            def _():
                copy_up(mu).wait_recv()

            @pl.when(p < last)
            def _():
                c, t, h = chunk_of(mu)
                mine = modes_ref[c, pl.ds(h * hc, hc)]
                up_out[mu] = jnp.where(plan_ref[1 + t] == p, mine, up_in[mu])
                copy_up(mu).start()

        md = step - quarter - (last - p)

        @pl.when(jnp.logical_and(md >= 0, md < chunks))
        def _():
            @pl.when(p < last)
            def _():
                copy_down(md).wait_recv()

            @pl.when(p > 0)
            def _():
                c, t, h = chunk_of(md)
                mine = modes_ref[c, pl.ds(h * hc, hc)]
                dn_out[md] = jnp.where(plan_ref[1 + t] == p, mine, dn_in[md])
                copy_down(md).start()

        mf = step - jnp.maximum(p, quarter + last - p)

        @pl.when(jnp.logical_and(mf >= 0, mf < chunks))
        def _():
            c, t, h = chunk_of(mf)
            mine = modes_ref[c, pl.ds(h * hc, hc)]
            owner = plan_ref[1 + t]
            got = jnp.where(owner < p, up_in[mf], dn_in[mf])
            tests[mf, q] = jnp.where(owner == p, mine, got)
            copy_side(mf).start()

        return carry

    lax.fori_loop(0, ticks, tick, 0)

    halo_up.wait_recv()
    halo_down.wait_recv()

    @pl.when(not_src)
    def _():
        def take(a, carry):
            copy_adv_side((1 - q) * quarter + a).wait_recv()
            return carry
        lax.fori_loop(0, quarter, take, 0)

    def values_step(xp, carry):
        values_of(xp)
        return carry

    lax.fori_loop(0, pairs, values_step, 0)

    def take_side(m, carry):
        copy_side(m).wait_recv()
        return carry

    lax.fori_loop(0, chunks, take_side, 0)
    acc[...] = jnp.zeros_like(acc)

    def gemm(kb, carry):
        c = kb // pairs
        xp = lax.rem(kb, pairs)
        for e in range(2):
            xy = 2 * xp + e
            h = xy // hc
            xl = lax.rem(xy, hc)
            weight = weights_ref[pl.ds(xy, 1), :]
            for t in range(NPANEL):
                for s in range(2):
                    raw = tests[(c * NPANEL + t) * halves + h, s, xl].astype(F32)
                    r = (t * 2 + s) * nm
                    wts[r : r + nm, e * lanes : (e + 1) * lanes] = (weight * raw).astype(BF16)
        acc[...] += lax.dot_general(vals[kb], wts[...], (((1,), (1,)), ((), ())), preferred_element_type=F32)
        return carry

    lax.fori_loop(0, comps * pairs, gemm, 0)

    for jt in range(nm * nm // lanes):
        turned = acc[jt * lanes : (jt + 1) * lanes, :].T
        for s in range(spaces):
            piece = turned[s * own_rows : (s + 1) * own_rows]
            tot[s, :, jt * lanes : (jt + 1) * lanes] = piece
            stage[s, :, jt * lanes : (jt + 1) * lanes] = piece.astype(BF16)

    copies = []
    for d in range(1, spaces):
        peer = lax.rem(me + d, spaces)
        copies.append(pltpu.make_async_remote_copy(
            src_ref=stage.at[peer], dst_ref=rs_in.at[d - 1], send_sem=rs_send.at[d - 1],
            recv_sem=rs_recv.at[d - 1], device_id={"space": peer}, device_id_type=MESH))
    for copy in copies:
        copy.start()

    halo_up.wait_send()
    halo_down.wait_send()

    @pl.when(is_src)
    def _():
        for a in range(pairs):
            copy_adv_side(a).wait_send()

    @pl.when(p < last)
    def _():
        def done(a, carry):
            copy_adv_side(q * quarter + a).wait_send()
            return carry
        lax.fori_loop(0, quarter, done, 0)

        def done_up(m, carry):
            copy_up(m).wait_send()
            return carry
        lax.fori_loop(0, chunks, done_up, 0)

    @pl.when(p > 0)
    def _():
        def done(a, carry):
            copy_adv_down(a).wait_send()
            return carry
        lax.fori_loop(0, quarter, done, 0)

        def done_down(m, carry):
            copy_down(m).wait_send()
            return carry
        lax.fori_loop(0, chunks, done_down, 0)

    def done_side(m, carry):
        copy_side(m).wait_send()
        return carry

    lax.fori_loop(0, chunks, done_side, 0)

    total = tot[me]
    for d, copy in enumerate(copies):
        copy.wait_recv()
        total = total + rs_in[d].astype(F32)
    out_ref[...] = total
    for copy in copies:
        copy.wait_send()


def solution(mesh):
    nmode, spaces = mesh.shape["mode"], mesh.shape["space"]

    def local(modes, weights, plan):
        comps, nm, nx, cy, lanes = modes.shape
        cells = nx * cy
        assert PANEL == 2 * nm and nmode % 2 == 0
        test_count = NPANEL * PANEL
        own_rows = test_count // spaces
        turned = modes.transpose(0, 2, 3, 1, 4).reshape(comps, cells, nm, lanes)
        hc, pairs = cells // 2, cells // 2
        chunks = comps * NPANEL * 2
        quarter = pairs // 2
        vm = pl.BlockSpec(memory_space=pltpu.VMEM)
        chunk = (chunks, hc, nm, lanes)
        dma = pltpu.SemaphoreType.DMA
        out = pl.pallas_call(
            functools.partial(kernel, (nmode // 2, spaces, cy, own_rows)),
            out_shape=jax.ShapeDtypeStruct((own_rows, nm * nm), F32),
            in_specs=[pl.BlockSpec(memory_space=pltpu.SMEM), vm, vm],
            out_specs=vm,
            scratch_shapes=[
                pltpu.VMEM((comps, cells + 2 * cy, nm, lanes), BF16),
                pltpu.VMEM((pairs, comps, 2, nm, lanes), BF16),
                pltpu.VMEM(chunk, BF16), pltpu.VMEM(chunk, BF16), pltpu.VMEM(chunk, BF16), pltpu.VMEM(chunk, BF16),
                pltpu.VMEM((chunks, 2, hc, nm, lanes), BF16),
                pltpu.VMEM((2, comps, nm, lanes), F32),
                pltpu.VMEM((comps * pairs, nm * nm, 2 * lanes), BF16),
                pltpu.VMEM((test_count, 2 * lanes), BF16),
                pltpu.VMEM((nm * nm, test_count), F32),
                pltpu.VMEM((spaces, own_rows, nm * nm), F32),
                pltpu.VMEM((spaces, own_rows, nm * nm), BF16),
                pltpu.VMEM((spaces - 1, own_rows, nm * nm), BF16),
                dma((2,)), dma((2,)),
                dma((chunks,)), dma((chunks,)), dma((chunks,)), dma((chunks,)), dma((chunks,)), dma((chunks,)),
                dma((quarter,)), dma((pairs,)), dma((pairs,)),
                dma((spaces - 1,)), dma((spaces - 1,)),
            ],
            compiler_params=pltpu.CompilerParams(
                collective_id=0, has_side_effects=True, vmem_limit_bytes=48 * 1024 * 1024),
        )(plan, turned, weights.reshape(cells, lanes))
        return out.reshape(own_rows, nm, nm)

    in_specs = (P(None, "mode", "space", None, None), P("space", None, None), P())
    return jax.shard_map(local, mesh=mesh, in_specs=in_specs, out_specs=P("space", None, "mode"), check_vma=False)
```

time: 219 us -> 84.6 us (0.39)
  waiting for transfers between devices: 127 us -> 0 us
  Pallas kernels: 0 us -> 81.6 us
  other arithmetic: 28.3 us -> 0 us
  local copies, waits for them, and re-layouts: 30.7 us -> 2.72 us
  between operations: 15.5 us -> 0.03 us
  matrix products: 13.5 us -> 0 us
  starting transfers between devices: 2.87 us -> 0 us
    psum x1 -> x0, waiting for transfers between devices: 96.4 us -> none  [broadcast(): return lax.psum(kept, axis)]
    pallas_call x0 -> x1, Pallas kernels: none -> 81.6 us  [local(): pl.pallas_call(functools.partial(kernel, (nmode // 2, spaces, cy, own_row...]
    reduce_scatter x1 -> x0, waiting for transfers between devices: 30.2 us -> none  [local(): lax.psum_scatter(product.reshape(own_rows * lax.axis_size('space'), local...]
    reshape x1, local copies, waits for them, and re-layouts: 21.2 us -> 0.97 us  [local(): return out.reshape(own_rows, nm, nm)]
    dot_general x1 -> x0, matrix products: 13.5 us -> none  [local(): lax.dot_general(weighted, stacked, (((0, 2), (0, 2)), ((), ())), preferre...]
    another operation x1 -> x0, other arithmetic: 11.5 us -> none  [local(): stacked = jnp.stack(slabs, axis=3)]
    convert_element_type x5 -> x0, other arithmetic: 11.2 us -> none  [the longest x4 10.1 us: local(): slabs.append(values.astype(jnp.bfloat16))]
    concatenate x4 -> x0, local copies, waits for them, and re-layouts: 4.16 us -> none  [local(): tests = jnp.concatenate(pieces, axis=1)]
  transfers between devices with their start and end apart: 4 -> 0, of which waited for: 2 -> 0; matrix products, arithmetic and copies ran while one was open for 5% -> 0% of each run, Pallas kernels for 0% -> 0%
where the time goes in v1:
time: 84.6 us; the launch traced here: 84.4 us
  Pallas kernels  81.6 us (96%)
  local copies, waits for them, and re-layouts  2.72 us (3%)
    pallas_call x1, Pallas kernels, local(): pl.pallas_call(functools.partial(kernel, (nmode // 2, spaces, cy, own_row...  81.6 us

profile of v1, /device:TPU:1, one launch (start us, length us, event | category | flops | bytes accessed | tf_op | source)
XLA Modules:
  0.0 84.4 jit_solution(4554039476479163304)
XLA Ops:
  0.0 0.0 copy-start
  0.0 1.1 %copy.4 = bf16[3,4,4,32,128]{4,3,2,1,0:T(8,128)(2,1)S(1)} copy(bf16[3,4,4,32,128]{4,2,1,3,0:T(4,128)(2,1)} %bitcast.5) | data formatting | bytes 786432 | tf_op jit(solution)/shard_map/transpose | solution.py:320
  1.1 0.0 copy-start.1
  1.1 0.0 copy-done
  1.1 0.6 copy-done.1
  1.8 81.6 %shard_map.37 = f32[32,1024]{1,0:T(8,128)S(1)} custom-call(s32[3]{0:T(128)S(1)} %copy-done.1, bf16[3,16,32,128]{3,2,1,0:T(8,128)(2,1)S(1)} %bitcast.3, f32[16,128]{1,0:T(8,128)S(1)} %bitcast.4), custom_call_target="tpu_custom_call" | custom-call | tf_op jit(solution)/shard_map/pallas_call | solution.py:327
  83.4 1.0 %reshape.11 = f32[32,32,32]{2,1,0:T(8,128)} reshape(f32[32,1024]{1,0:T(8,128)S(1)} %shard_map.37) | data formatting | bytes 262144 | tf_op jit(solution)/shard_map/reshape | solution.py:352
Async XLA Ops:
  0.0 1.1 %copy-start = (f32[4,4,128]{2,1,0:T(4,128)S(1)}, f32[4,4,128]{2,1,0:T(4,128)}, u32[]{:S(2)}) copy-start(f32[4,4,128]{2,1,0:T(4,128)} %param.4) | copy-start | bytes 24580
  1.1 0.7 copy-start.1

commit v2 on v1

--- a/solution.py
+++ b/solution.py
@@ -9,6 +9,7 @@
 
 PANEL = 64
 NPANEL = 2
+SKEW = 3
 MESH = pl.DeviceIdType.MESH
 F32 = jnp.float32
 BF16 = jnp.bfloat16
@@ -46,8 +47,8 @@
 
     def chunk_of(m):
         c = m // (NPANEL * halves)
-        t = lax.rem(m // halves, NPANEL)
-        h = lax.rem(m, halves)
+        h = lax.rem(m // NPANEL, halves)
+        t = lax.rem(m, NPANEL)
         return c, t, h
 
     ext[:, cy : cy + cells] = modes_ref[...]
@@ -60,13 +61,13 @@
     @pl.when(p == 0)
     def _():
         for m in range(chunks):
-            c, t, h = m // (NPANEL * halves), (m // halves) % NPANEL, m % halves
+            c, h = m // (NPANEL * halves), (m // NPANEL) % halves
             up_in[m] = modes_ref[c, h * hc : (h + 1) * hc]
 
     @pl.when(p == last)
     def _():
         for m in range(chunks):
-            c, t, h = m // (NPANEL * halves), (m // halves) % NPANEL, m % halves
+            c, h = m // (NPANEL * halves), (m // NPANEL) % halves
             dn_in[m] = modes_ref[c, h * hc : (h + 1) * hc]
 
     pl.semaphore_wait(barrier, 3 + spaces - 1)
@@ -140,10 +141,35 @@
 
             lax.fori_loop(0, nm, row, 0, unroll=4)
 
-    ticks = chunks + quarter + last + 1
+    def gemm(kb):
+        c = kb // (pairs // 2)
+        h = lax.rem(kb // (quarter // 2), halves)
+        total = None
+        for k in range(2):
+            xp = lax.rem(kb, pairs // 2) * 2 + k
+            for e in range(2):
+                xy = 2 * xp + e
+                xl = lax.rem(xy, hc)
+                weight = weights_ref[pl.ds(xy, 1), :]
+                for t in range(NPANEL):
+                    for s in range(2):
+                        raw = tests[(c * halves + h) * NPANEL + t, s, xl].astype(F32)
+                        r = (t * 2 + s) * nm
+                        wts[k, r : r + nm, e * lanes : (e + 1) * lanes] = (weight * raw).astype(BF16)
+            part = lax.dot_general(vals[c * pairs + xp], wts[k], (((1,), (1,)), ((), ())), preferred_element_type=F32)
+            total = part if total is None else total + part
+        acc[...] += total
+
+    off_up = SKEW * p
+    off_adv = SKEW * (last - p)
+    off_down = quarter + off_adv
+    off_own = jnp.maximum(off_up, off_down)
+    off_dot = off_own + 1 + SKEW
+    ticks = quarter + SKEW * last + 1 + SKEW + chunks
+    acc[...] = jnp.zeros_like(acc)
 
     def tick(step, carry):
-        a = step - (last - p)
+        a = step - off_adv
 
         @pl.when(jnp.logical_and(a >= 0, a < quarter))
         def _():
@@ -159,7 +185,7 @@
             def _():
                 copy_adv_side(q * quarter + a).start()
 
-        mu = step - p
+        mu = step - off_up
 
         @pl.when(jnp.logical_and(mu >= 0, mu < chunks))
         def _():
@@ -174,7 +200,7 @@
                 up_out[mu] = jnp.where(plan_ref[1 + t] == p, mine, up_in[mu])
                 copy_up(mu).start()
 
-        md = step - quarter - (last - p)
+        md = step - off_down
 
         @pl.when(jnp.logical_and(md >= 0, md < chunks))
         def _():
@@ -189,7 +215,7 @@
                 dn_out[md] = jnp.where(plan_ref[1 + t] == p, mine, dn_in[md])
                 copy_down(md).start()
 
-        mf = step - jnp.maximum(p, quarter + last - p)
+        mf = step - off_own
 
         @pl.when(jnp.logical_and(mf >= 0, mf < chunks))
         def _():
@@ -200,50 +226,35 @@
             tests[mf, q] = jnp.where(owner == p, mine, got)
             copy_side(mf).start()
 
+        @pl.when(jnp.logical_and(a >= 0, a < pairs))
+        def _():
+            @pl.when(a == 0)
+            def _():
+                halo_up.wait_recv()
+                halo_down.wait_recv()
+
+            xp = lax.rem(q * quarter + a, pairs)
+
+            @pl.when(jnp.logical_and(a >= quarter, not_src))
+            def _():
+                copy_adv_side(xp).wait_recv()
+
+            values_of(xp)
+
+        mg = step - off_dot
+
+        @pl.when(jnp.logical_and(mg >= 0, mg < chunks))
+        def _():
+            @pl.when(lax.rem(mg, 2) == 0)
+            def _():
+                copy_side(mg).wait_recv()
+                copy_side(mg + 1).wait_recv()
+
+            gemm(mg)
+
         return carry
 
     lax.fori_loop(0, ticks, tick, 0)
-
-    halo_up.wait_recv()
-    halo_down.wait_recv()
-
-    @pl.when(not_src)
-    def _():
-        def take(a, carry):
-            copy_adv_side((1 - q) * quarter + a).wait_recv()
-            return carry
-        lax.fori_loop(0, quarter, take, 0)
-
-    def values_step(xp, carry):
-        values_of(xp)
-        return carry
-
-    lax.fori_loop(0, pairs, values_step, 0)
-
-    def take_side(m, carry):
-        copy_side(m).wait_recv()
-        return carry
-
-    lax.fori_loop(0, chunks, take_side, 0)
-    acc[...] = jnp.zeros_like(acc)
-
-    def gemm(kb, carry):
-        c = kb // pairs
-        xp = lax.rem(kb, pairs)
-        for e in range(2):
-            xy = 2 * xp + e
-            h = xy // hc
-            xl = lax.rem(xy, hc)
-            weight = weights_ref[pl.ds(xy, 1), :]
-            for t in range(NPANEL):
-                for s in range(2):
-                    raw = tests[(c * NPANEL + t) * halves + h, s, xl].astype(F32)
-                    r = (t * 2 + s) * nm
-                    wts[r : r + nm, e * lanes : (e + 1) * lanes] = (weight * raw).astype(BF16)
-        acc[...] += lax.dot_general(vals[kb], wts[...], (((1,), (1,)), ((), ())), preferred_element_type=F32)
-        return carry
-
-    lax.fori_loop(0, comps * pairs, gemm, 0)
 
     for jt in range(nm * nm // lanes):
         turned = acc[jt * lanes : (jt + 1) * lanes, :].T
@@ -336,7 +347,7 @@
                 pltpu.VMEM((chunks, 2, hc, nm, lanes), BF16),
                 pltpu.VMEM((2, comps, nm, lanes), F32),
                 pltpu.VMEM((comps * pairs, nm * nm, 2 * lanes), BF16),
-                pltpu.VMEM((test_count, 2 * lanes), BF16),
+                pltpu.VMEM((2, test_count, 2 * lanes), BF16),
                 pltpu.VMEM((nm * nm, test_count), F32),
                 pltpu.VMEM((spaces, own_rows, nm * nm), F32),
                 pltpu.VMEM((spaces, own_rows, nm * nm), BF16),

time: 84.6 us -> 51.5 us (0.61)
  Pallas kernels: 81.6 us -> 48.6 us
    pallas_call x1, Pallas kernels: 81.6 us -> 48.6 us  [local(): pl.pallas_call(functools.partial(kernel, (nmode // 2, spaces, cy, own_row...]
where the time goes in v2:
time: 51.5 us; the launch traced here: 51.4 us
  Pallas kernels  48.6 us (94%)
  local copies, waits for them, and re-layouts  2.72 us (5%)
    pallas_call x1, Pallas kernels, local(): pl.pallas_call(functools.partial(kernel, (nmode // 2, spaces, cy, own_row...  48.6 us
    transpose x1, local copies, waits for them, and re-layouts, local(): turned = modes.transpose(0, 2, 3, 1, 4).reshape(comps, cells, nm, lanes)  1.11 us

profile of v2, /device:TPU:1, one launch (start us, length us, event | category | flops | bytes accessed | tf_op | source)
XLA Modules:
  0.0 51.4 jit_solution(2815357457188328552)
XLA Ops:
  0.0 0.0 copy-start
  0.0 1.1 %copy.4 = bf16[3,4,4,32,128]{4,3,2,1,0:T(8,128)(2,1)S(1)} copy(bf16[3,4,4,32,128]{4,2,1,3,0:T(4,128)(2,1)} %bitcast.5) | data formatting | bytes 786432 | tf_op jit(solution)/shard_map/transpose | solution.py:331
  1.1 0.0 copy-start.1
  1.1 0.0 copy-done
  1.1 0.6 %copy-done.1 = s32[3]{0:T(128)S(1)} copy-done((s32[3]{0:T(128)S(1)}, s32[3]{0:T(128)}, u32[]{:S(2)}) %copy-start.1) | copy-done | bytes 36
  1.8 48.6 %shard_map.37 = f32[32,1024]{1,0:T(8,128)S(1)} custom-call(s32[3]{0:T(128)S(1)} %copy-done.1, bf16[3,16,32,128]{3,2,1,0:T(8,128)(2,1)S(1)} %bitcast.3, f32[16,128]{1,0:T(8,128)S(1)} %bitcast.4), custom_call_target="tpu_custom_call" | custom-call | tf_op jit(solution)/shard_map/pallas_call | solution.py:338
  50.4 1.0 %reshape.11 = f32[32,32,32]{2,1,0:T(8,128)} reshape(f32[32,1024]{1,0:T(8,128)S(1)} %shard_map.37) | data formatting | bytes 262144 | tf_op jit(solution)/shard_map/reshape | solution.py:363
Async XLA Ops:
  0.0 1.1 %copy-start = (f32[4,4,128]{2,1,0:T(4,128)S(1)}, f32[4,4,128]{2,1,0:T(4,128)}, u32[]{:S(2)}) copy-start(f32[4,4,128]{2,1,0:T(4,128)} %param.4) | copy-start | bytes 24580
  1.1 0.7 %copy-start.1 = (s32[3]{0:T(128)S(1)}, s32[3]{0:T(128)}, u32[]{:S(2)}) copy-start(s32[3]{0:T(128)} %plan_ref.1) | copy-start | bytes 40

commit v3 on v2

--- a/solution.py
+++ b/solution.py
@@ -10,6 +10,8 @@
 PANEL = 64
 NPANEL = 2
 SKEW = 3
+TAIL = 4
+LEAD = 2
 MESH = pl.DeviceIdType.MESH
 F32 = jnp.float32
 BF16 = jnp.bfloat16
@@ -20,10 +22,9 @@
            halo_send, halo_recv, up_send, up_recv, dn_send, dn_recv, y_send, y_recv,
            ad_send, ay_send, adv_recv, rs_send, rs_recv):
     panels, spaces, cy, own_rows = dims
-    comps, cells, nm, lanes = modes_ref.shape
-    halves = 2
-    hc = cells // halves
-    chunks = comps * NPANEL * halves
+    chunks, _, nm, lanes = modes_ref.shape
+    nx = weights_ref.shape[0]
+    comps, cells = chunks // nx, nx * cy
     pairs = cells // 2
     quarter = pairs // 2
     last = panels - 1
@@ -40,37 +41,43 @@
     not_src = jnp.logical_or(p < last, q == 0)
 
     barrier = pltpu.get_barrier_semaphore()
-    for other in (partner, below, above):
-        pl.semaphore_signal(barrier, inc=1, device_id={"mode": other}, device_id_type=MESH)
+    pl.semaphore_signal(barrier, inc=1, device_id={"mode": partner}, device_id_type=MESH)
+
+    @pl.when(p > 0)
+    def _():
+        pl.semaphore_signal(barrier, inc=1, device_id={"mode": below}, device_id_type=MESH)
+
+    @pl.when(p < last)
+    def _():
+        pl.semaphore_signal(barrier, inc=1, device_id={"mode": above}, device_id_type=MESH)
+
     for d in range(1, spaces):
         pl.semaphore_signal(barrier, inc=1, device_id={"space": lax.rem(me + d, spaces)}, device_id_type=MESH)
 
-    def chunk_of(m):
-        c = m // (NPANEL * halves)
-        h = lax.rem(m // NPANEL, halves)
-        t = lax.rem(m, NPANEL)
-        return c, t, h
-
-    ext[:, cy : cy + cells] = modes_ref[...]
+    for m in range(chunks):
+        first = cy * (1 + m % nx)
+        ext[m // nx, first : first + cy] = modes_ref[m]
 
     @pl.when(is_src)
     def _():
         for a in range(pairs):
-            advb[a] = modes_ref[:, 2 * a : 2 * a + 2]
+            for c in range(comps):
+                at = 2 * a % cy
+                advb[a, c] = modes_ref[c * nx + 2 * a // cy, at : at + 2]
 
     @pl.when(p == 0)
     def _():
         for m in range(chunks):
-            c, h = m // (NPANEL * halves), (m // NPANEL) % halves
-            up_in[m] = modes_ref[c, h * hc : (h + 1) * hc]
+            for t in range(NPANEL):
+                up_in[m, t] = modes_ref[m]
 
     @pl.when(p == last)
     def _():
         for m in range(chunks):
-            c, h = m // (NPANEL * halves), (m // NPANEL) % halves
-            dn_in[m] = modes_ref[c, h * hc : (h + 1) * hc]
-
-    pl.semaphore_wait(barrier, 3 + spaces - 1)
+            for t in range(NPANEL):
+                dn_in[m, t] = modes_ref[m]
+
+    pl.semaphore_wait(barrier, spaces + (p > 0).astype(jnp.int32) + (p < last).astype(jnp.int32))
 
     def copy_adv_down(a):
         return pltpu.make_async_remote_copy(
@@ -104,21 +111,22 @@
         for a in range(pairs):
             copy_adv_side(a).start()
 
-    halo_up = pltpu.make_async_remote_copy(
-        src_ref=modes_ref.at[:, pl.ds(cells - cy, cy)], dst_ref=ext.at[:, pl.ds(0, cy)],
-        send_sem=halo_send.at[0], recv_sem=halo_recv.at[0], device_id={"space": right}, device_id_type=MESH)
-    halo_down = pltpu.make_async_remote_copy(
-        src_ref=modes_ref.at[:, pl.ds(0, cy)], dst_ref=ext.at[:, pl.ds(cells + cy, cy)],
-        send_sem=halo_send.at[1], recv_sem=halo_recv.at[1], device_id={"space": left}, device_id_type=MESH)
-    halo_up.start()
-    halo_down.start()
+    halos = []
+    for c in range(comps):
+        for k, (plane, at, peer) in enumerate(((nx - 1, 0, right), (0, cells + cy, left))):
+            halos.append(pltpu.make_async_remote_copy(
+                src_ref=modes_ref.at[c * nx + plane], dst_ref=ext.at[c, pl.ds(at, cy)],
+                send_sem=halo_send.at[c, k], recv_sem=halo_recv.at[c, k],
+                device_id={"space": peer}, device_id_type=MESH))
+    for halo in halos:
+        halo.start()
 
     def values_of(xp):
         adv_at = advb.at[xp]
         for e in range(2):
             xy = 2 * xp + e
-            x = xy // cy
-            y = lax.rem(xy, cy)
+            x = lax.div(xp, cy // 2)
+            y = xy - x * cy
             y_next = cy + x * cy + lax.rem(y + 1, cy)
             y_prev = cy + x * cy + lax.rem(y + cy - 1, cy)
             for d in range(3):
@@ -141,22 +149,18 @@
 
             lax.fori_loop(0, nm, row, 0, unroll=4)
 
-    def gemm(kb):
-        c = kb // (pairs // 2)
-        h = lax.rem(kb // (quarter // 2), halves)
+    def gemm(m):
+        plane = lax.rem(m, nx)
         total = None
-        for k in range(2):
-            xp = lax.rem(kb, pairs // 2) * 2 + k
+        for k in range(cy // 2):
             for e in range(2):
-                xy = 2 * xp + e
-                xl = lax.rem(xy, hc)
-                weight = weights_ref[pl.ds(xy, 1), :]
+                weight = weights_ref[plane, 2 * k + e : 2 * k + e + 1, :]
                 for t in range(NPANEL):
                     for s in range(2):
-                        raw = tests[(c * halves + h) * NPANEL + t, s, xl].astype(F32)
+                        raw = tests[m, s, t, 2 * k + e].astype(F32)
                         r = (t * 2 + s) * nm
                         wts[k, r : r + nm, e * lanes : (e + 1) * lanes] = (weight * raw).astype(BF16)
-            part = lax.dot_general(vals[c * pairs + xp], wts[k], (((1,), (1,)), ((), ())), preferred_element_type=F32)
+            part = lax.dot_general(vals[m * (cy // 2) + k], wts[k], (((1,), (1,)), ((), ())), preferred_element_type=F32)
             total = part if total is None else total + part
         acc[...] += total
 
@@ -164,12 +168,12 @@
     off_adv = SKEW * (last - p)
     off_down = quarter + off_adv
     off_own = jnp.maximum(off_up, off_down)
-    off_dot = off_own + 1 + SKEW
-    ticks = quarter + SKEW * last + 1 + SKEW + chunks
+    off_dot = off_own + TAIL
+    ticks = quarter + SKEW * last + TAIL + chunks
     acc[...] = jnp.zeros_like(acc)
 
     def tick(step, carry):
-        a = step - off_adv
+        a = step - off_adv - LEAD
 
         @pl.when(jnp.logical_and(a >= 0, a < quarter))
         def _():
@@ -195,14 +199,15 @@
 
             @pl.when(p < last)
             def _():
-                c, t, h = chunk_of(mu)
-                mine = modes_ref[c, pl.ds(h * hc, hc)]
-                up_out[mu] = jnp.where(plan_ref[1 + t] == p, mine, up_in[mu])
+                mine = modes_ref[mu]
+                for t in range(NPANEL):
+                    up_out[mu, t] = jnp.where(plan_ref[1 + t] == p, mine, up_in[mu, t])
                 copy_up(mu).start()
 
-        md = step - off_down
-
-        @pl.when(jnp.logical_and(md >= 0, md < chunks))
+        early = step - off_adv
+        md = jnp.where(early < LEAD, early, step - off_down)
+
+        @pl.when(jnp.logical_and(md >= jnp.where(early < LEAD, 0, LEAD), md < chunks))
         def _():
             @pl.when(p < last)
             def _():
@@ -210,28 +215,28 @@
 
             @pl.when(p > 0)
             def _():
-                c, t, h = chunk_of(md)
-                mine = modes_ref[c, pl.ds(h * hc, hc)]
-                dn_out[md] = jnp.where(plan_ref[1 + t] == p, mine, dn_in[md])
+                mine = modes_ref[md]
+                for t in range(NPANEL):
+                    dn_out[md, t] = jnp.where(plan_ref[1 + t] == p, mine, dn_in[md, t])
                 copy_down(md).start()
 
         mf = step - off_own
 
         @pl.when(jnp.logical_and(mf >= 0, mf < chunks))
         def _():
-            c, t, h = chunk_of(mf)
-            mine = modes_ref[c, pl.ds(h * hc, hc)]
-            owner = plan_ref[1 + t]
-            got = jnp.where(owner < p, up_in[mf], dn_in[mf])
-            tests[mf, q] = jnp.where(owner == p, mine, got)
+            mine = modes_ref[mf]
+            for t in range(NPANEL):
+                owner = plan_ref[1 + t]
+                got = jnp.where(owner < p, up_in[mf, t], dn_in[mf, t])
+                tests[mf, q, t] = jnp.where(owner == p, mine, got)
             copy_side(mf).start()
 
         @pl.when(jnp.logical_and(a >= 0, a < pairs))
         def _():
             @pl.when(a == 0)
             def _():
-                halo_up.wait_recv()
-                halo_down.wait_recv()
+                for halo in halos:
+                    halo.wait_recv()
 
             xp = lax.rem(q * quarter + a, pairs)
 
@@ -245,11 +250,7 @@
 
         @pl.when(jnp.logical_and(mg >= 0, mg < chunks))
         def _():
-            @pl.when(lax.rem(mg, 2) == 0)
-            def _():
-                copy_side(mg).wait_recv()
-                copy_side(mg + 1).wait_recv()
-
+            copy_side(mg).wait_recv()
             gemm(mg)
 
         return carry
@@ -272,8 +273,8 @@
     for copy in copies:
         copy.start()
 
-    halo_up.wait_send()
-    halo_down.wait_send()
+    for halo in halos:
+        halo.wait_send()
 
     @pl.when(is_src)
     def _():
@@ -328,12 +329,12 @@
         assert PANEL == 2 * nm and nmode % 2 == 0
         test_count = NPANEL * PANEL
         own_rows = test_count // spaces
-        turned = modes.transpose(0, 2, 3, 1, 4).reshape(comps, cells, nm, lanes)
-        hc, pairs = cells // 2, cells // 2
-        chunks = comps * NPANEL * 2
+        turned = modes.transpose(0, 2, 3, 1, 4).reshape(comps * nx, cy, nm, lanes)
+        pairs = cells // 2
+        chunks = comps * nx
         quarter = pairs // 2
         vm = pl.BlockSpec(memory_space=pltpu.VMEM)
-        chunk = (chunks, hc, nm, lanes)
+        chunk = (chunks, NPANEL, cy, nm, lanes)
         dma = pltpu.SemaphoreType.DMA
         out = pl.pallas_call(
             functools.partial(kernel, (nmode // 2, spaces, cy, own_rows)),
@@ -344,22 +345,22 @@
                 pltpu.VMEM((comps, cells + 2 * cy, nm, lanes), BF16),
                 pltpu.VMEM((pairs, comps, 2, nm, lanes), BF16),
                 pltpu.VMEM(chunk, BF16), pltpu.VMEM(chunk, BF16), pltpu.VMEM(chunk, BF16), pltpu.VMEM(chunk, BF16),
-                pltpu.VMEM((chunks, 2, hc, nm, lanes), BF16),
+                pltpu.VMEM((chunks, 2, NPANEL, cy, nm, lanes), BF16),
                 pltpu.VMEM((2, comps, nm, lanes), F32),
                 pltpu.VMEM((comps * pairs, nm * nm, 2 * lanes), BF16),
-                pltpu.VMEM((2, test_count, 2 * lanes), BF16),
+                pltpu.VMEM((cy // 2, test_count, 2 * lanes), BF16),
                 pltpu.VMEM((nm * nm, test_count), F32),
                 pltpu.VMEM((spaces, own_rows, nm * nm), F32),
                 pltpu.VMEM((spaces, own_rows, nm * nm), BF16),
                 pltpu.VMEM((spaces - 1, own_rows, nm * nm), BF16),
-                dma((2,)), dma((2,)),
+                dma((comps, 2)), dma((comps, 2)),
                 dma((chunks,)), dma((chunks,)), dma((chunks,)), dma((chunks,)), dma((chunks,)), dma((chunks,)),
                 dma((quarter,)), dma((pairs,)), dma((pairs,)),
                 dma((spaces - 1,)), dma((spaces - 1,)),
             ],
             compiler_params=pltpu.CompilerParams(
                 collective_id=0, has_side_effects=True, vmem_limit_bytes=48 * 1024 * 1024),
-        )(plan, turned, weights.reshape(cells, lanes))
+        )(plan, turned, weights)
         return out.reshape(own_rows, nm, nm)
 
     in_specs = (P(None, "mode", "space", None, None), P("space", None, None), P())

time: 51.5 us -> 49.2 us (0.955)
  Pallas kernels: 48.6 us -> 46.3 us
    pallas_call x1, Pallas kernels: 48.6 us -> 46.3 us  [local(): pl.pallas_call(functools.partial(kernel, (nmode // 2, spaces, cy, own_row...]
where the time goes in v3:
time: 49.2 us; the launch traced here: 49 us
  Pallas kernels  46.3 us (94%)
  local copies, waits for them, and re-layouts  2.72 us (6%)
    pallas_call x1, Pallas kernels, local(): pl.pallas_call(functools.partial(kernel, (nmode // 2, spaces, cy, own_row...  46.3 us
    transpose x1, local copies, waits for them, and re-layouts, local(): turned = modes.transpose(0, 2, 3, 1, 4).reshape(comps * nx, cy, nm, lanes)  1.11 us

profile of v3, /device:TPU:1, one launch (start us, length us, event | category | flops | bytes accessed | tf_op | source)
XLA Modules:
  0.0 49.0 jit_solution(6411640815277063674)
XLA Ops:
  0.0 0.0 copy-start
  0.0 1.1 %copy.4 = bf16[3,4,4,32,128]{4,3,2,1,0:T(8,128)(2,1)S(1)} copy(bf16[3,4,4,32,128]{4,2,1,3,0:T(4,128)(2,1)} %bitcast.3) | data formatting | bytes 786432 | tf_op jit(solution)/shard_map/transpose | solution.py:332
  1.1 0.0 copy-start.1
  1.1 0.0 copy-done
  1.1 0.6 %copy-done.1 = s32[3]{0:T(128)S(1)} copy-done((s32[3]{0:T(128)S(1)}, s32[3]{0:T(128)}, u32[]{:S(2)}) %copy-start.1) | copy-done | bytes 36
  1.8 46.3 %shard_map.37 = f32[32,1024]{1,0:T(8,128)S(1)} custom-call(s32[3]{0:T(128)S(1)} %copy-done.1, bf16[12,4,32,128]{3,2,1,0:T(8,128)(2,1)S(1)} %bitcast.2, f32[4,4,128]{2,1,0:T(4,128)S(1)} %copy-done), custom_call_target="tpu_custom_call" | custom-call | tf_op jit(solution)/shard_map/pallas_call | solution.py:339
  48.1 1.0 %reshape.7 = f32[32,32,32]{2,1,0:T(8,128)} reshape(f32[32,1024]{1,0:T(8,128)S(1)} %shard_map.37) | data formatting | bytes 262144 | tf_op jit(solution)/shard_map/reshape | solution.py:364
Async XLA Ops:
  0.0 1.1 %copy-start = (f32[4,4,128]{2,1,0:T(4,128)S(1)}, f32[4,4,128]{2,1,0:T(4,128)}, u32[]{:S(2)}) copy-start(f32[4,4,128]{2,1,0:T(4,128)} %weights_ref.1) | copy-start | bytes 24580
  1.1 0.7 %copy-start.1 = (s32[3]{0:T(128)S(1)}, s32[3]{0:T(128)}, u32[]{:S(2)}) copy-start(s32[3]{0:T(128)} %plan_ref.1) | copy-start | bytes 40

commit v4 on v3

--- a/solution.py
+++ b/solution.py
@@ -91,14 +91,14 @@
             send_sem=ay_send.at[x], recv_sem=adv_recv.at[x],
             device_id={"mode": partner}, device_id_type=MESH)
 
-    def copy_up(m):
-        return pltpu.make_async_remote_copy(
-            src_ref=up_out.at[m], dst_ref=up_in.at[m], send_sem=up_send.at[m], recv_sem=up_recv.at[m],
+    def copy_up(m, t):
+        return pltpu.make_async_remote_copy(
+            src_ref=up_out.at[m, t], dst_ref=up_in.at[m, t], send_sem=up_send.at[m, t], recv_sem=up_recv.at[m, t],
             device_id={"mode": above}, device_id_type=MESH)
 
-    def copy_down(m):
-        return pltpu.make_async_remote_copy(
-            src_ref=dn_out.at[m], dst_ref=dn_in.at[m], send_sem=dn_send.at[m], recv_sem=dn_recv.at[m],
+    def copy_down(m, t):
+        return pltpu.make_async_remote_copy(
+            src_ref=dn_out.at[m, t], dst_ref=dn_in.at[m, t], send_sem=dn_send.at[m, t], recv_sem=dn_recv.at[m, t],
             device_id={"mode": below}, device_id_type=MESH)
 
     def copy_side(m):
@@ -193,32 +193,30 @@
 
         @pl.when(jnp.logical_and(mu >= 0, mu < chunks))
         def _():
-            @pl.when(p > 0)
-            def _():
-                copy_up(mu).wait_recv()
-
-            @pl.when(p < last)
-            def _():
-                mine = modes_ref[mu]
-                for t in range(NPANEL):
-                    up_out[mu, t] = jnp.where(plan_ref[1 + t] == p, mine, up_in[mu, t])
-                copy_up(mu).start()
+            for t in range(NPANEL):
+                @pl.when(p > 0)
+                def _():
+                    copy_up(mu, t).wait_recv()
+
+                @pl.when(p < last)
+                def _():
+                    up_out[mu, t] = jnp.where(plan_ref[1 + t] == p, modes_ref[mu], up_in[mu, t])
+                    copy_up(mu, t).start()
 
         early = step - off_adv
         md = jnp.where(early < LEAD, early, step - off_down)
 
         @pl.when(jnp.logical_and(md >= jnp.where(early < LEAD, 0, LEAD), md < chunks))
         def _():
-            @pl.when(p < last)
-            def _():
-                copy_down(md).wait_recv()
-
-            @pl.when(p > 0)
-            def _():
-                mine = modes_ref[md]
-                for t in range(NPANEL):
-                    dn_out[md, t] = jnp.where(plan_ref[1 + t] == p, mine, dn_in[md, t])
-                copy_down(md).start()
+            for t in range(NPANEL):
+                @pl.when(p < last)
+                def _():
+                    copy_down(md, t).wait_recv()
+
+                @pl.when(p > 0)
+                def _():
+                    dn_out[md, t] = jnp.where(plan_ref[1 + t] == p, modes_ref[md], dn_in[md, t])
+                    copy_down(md, t).start()
 
         mf = step - off_own
 
@@ -289,7 +287,8 @@
         lax.fori_loop(0, quarter, done, 0)
 
         def done_up(m, carry):
-            copy_up(m).wait_send()
+            for t in range(NPANEL):
+                copy_up(m, t).wait_send()
             return carry
         lax.fori_loop(0, chunks, done_up, 0)
 
@@ -301,7 +300,8 @@
         lax.fori_loop(0, quarter, done, 0)
 
         def done_down(m, carry):
-            copy_down(m).wait_send()
+            for t in range(NPANEL):
+                copy_down(m, t).wait_send()
             return carry
         lax.fori_loop(0, chunks, done_down, 0)
 
@@ -354,7 +354,7 @@
                 pltpu.VMEM((spaces, own_rows, nm * nm), BF16),
                 pltpu.VMEM((spaces - 1, own_rows, nm * nm), BF16),
                 dma((comps, 2)), dma((comps, 2)),
-                dma((chunks,)), dma((chunks,)), dma((chunks,)), dma((chunks,)), dma((chunks,)), dma((chunks,)),
+                *[dma((chunks, NPANEL))] * 4, dma((chunks,)), dma((chunks,)),
                 dma((quarter,)), dma((pairs,)), dma((pairs,)),
                 dma((spaces - 1,)), dma((spaces - 1,)),
             ],

time: 49.2 us -> 49.6 us (level)
  no operation moved by 1% of the time
where the time goes in v4:
time: 49.6 us; the launch traced here: 49.5 us
  Pallas kernels  46.7 us (94%)
  local copies, waits for them, and re-layouts  2.72 us (5%)
    pallas_call x1, Pallas kernels, local(): pl.pallas_call(functools.partial(kernel, (nmode // 2, spaces, cy, own_row...  46.7 us
    transpose x1, local copies, waits for them, and re-layouts, local(): turned = modes.transpose(0, 2, 3, 1, 4).reshape(comps * nx, cy, nm, lanes)  1.11 us

profile of v4, /device:TPU:1, one launch (start us, length us, event | category | flops | bytes accessed | tf_op | source)
XLA Modules:
  0.0 49.5 jit_solution(5910697379829694039)
XLA Ops:
  0.0 0.0 copy-start
  0.0 1.1 %copy.4 = bf16[3,4,4,32,128]{4,3,2,1,0:T(8,128)(2,1)S(1)} copy(bf16[3,4,4,32,128]{4,2,1,3,0:T(4,128)(2,1)} %bitcast.3) | data formatting | bytes 786432 | tf_op jit(solution)/shard_map/transpose | solution.py:332
  1.1 0.0 copy-start.1
  1.1 0.0 copy-done
  1.1 0.6 %copy-done.1 = s32[3]{0:T(128)S(1)} copy-done((s32[3]{0:T(128)S(1)}, s32[3]{0:T(128)}, u32[]{:S(2)}) %copy-start.1) | copy-done | bytes 36
  1.8 46.7 %shard_map.37 = f32[32,1024]{1,0:T(8,128)S(1)} custom-call(s32[3]{0:T(128)S(1)} %copy-done.1, bf16[12,4,32,128]{3,2,1,0:T(8,128)(2,1)S(1)} %bitcast.2, f32[4,4,128]{2,1,0:T(4,128)S(1)} %copy-done), custom_call_target="tpu_custom_call" | custom-call | tf_op jit(solution)/shard_map/pallas_call | solution.py:339
  48.5 1.0 %reshape.7 = f32[32,32,32]{2,1,0:T(8,128)} reshape(f32[32,1024]{1,0:T(8,128)S(1)} %shard_map.37) | data formatting | bytes 262144 | tf_op jit(solution)/shard_map/reshape | solution.py:364
Async XLA Ops:
  0.0 1.1 %copy-start = (f32[4,4,128]{2,1,0:T(4,128)S(1)}, f32[4,4,128]{2,1,0:T(4,128)}, u32[]{:S(2)}) copy-start(f32[4,4,128]{2,1,0:T(4,128)} %weights_ref.1) | copy-start | bytes 24580
  1.1 0.7 %copy-start.1 = (s32[3]{0:T(128)S(1)}, s32[3]{0:T(128)}, u32[]{:S(2)}) copy-start(s32[3]{0:T(128)} %plan_ref.1) | copy-start | bytes 40
